TPU v7x, 512 devices: a whole 4x4x16 slice. The times are simulated.
512 devices in a mesh: cell: 128 (over z, x, core), lag: 4 (over y).
Axes of the slice: x: 4, y: 4, z: 16, core: 2. Of those that a mesh axis runs over, the one named last changes fastest.
Arguments:
- green: bfloat16 [32, 640, 32768], P('lag', None, 'cell'), may hold values from -0.0078125 to 0.0078125
- source: bfloat16 [8, 48, 32768], P(None, None, 'cell'), may hold values from -6 to 6
- observed: float32 [8, 48, 640], replicated, may hold values from -6 to 6
- lag_gaps: int32 [31], replicated, may hold values from 1 to 2, 47 in all
- huber_level: int32 [640], replicated, may hold values from 0 to 7
Outputs:
- gradient: float32 [8, 48, 32768], P(None, 'lag', 'cell')
Inputs may be any that keep to these rules, and one draw needn't show every extreme that they name: `lag_gaps`: the gaps sum to 47.
All inputs are finite; a program needn't handle non-finite values.
Results may differ from a plain program's by a relative error of at most 0.0034.
Values may be sent and summed in bfloat16 or wider, within the bound.
No kernel may reach another device: no remote copies, remote signals or barrier semaphores. Data moves between devices by JAX's collectives and lax.ppermute only.
A program may use at most 64 MiB of HBM per device.

v0:
```python
import jax
import jax.numpy as jnp
from jax import lax
from jax.sharding import PartitionSpec as P


def body(green, source, observed, lag_gaps, huber_level):
    rows, steps, cells = source.shape
    sensors = green.shape[1]
    own_count = green.shape[0]
    lag_table = jnp.concatenate([jnp.zeros((1,), jnp.int32), jnp.cumsum(lag_gaps)])
    first = lax.axis_index("lag") * own_count
    lag_of = lax.dynamic_slice_in_dim(lag_table, first, own_count, 0)
    padded = jnp.concatenate([jnp.zeros_like(source), source], axis=1)
    predicted = jnp.zeros((rows, steps, sensors), jnp.float32)
    for block in range(own_count):
        shifted = lax.dynamic_slice_in_dim(padded, steps - lag_of[block], steps, 1)
        predicted = predicted + jnp.einsum(
            "rtc,sc->rts", shifted, green[block], preferred_element_type=jnp.float32
        )
    threshold = 0.3 * (huber_level.astype(jnp.float32) + 1.0)
    summed = lax.psum(predicted, ("cell", "lag"))
    misfit = summed - observed
    weighted = (misfit * threshold / jnp.maximum(jnp.abs(misfit), threshold)).astype(jnp.bfloat16)
    later = jnp.concatenate([weighted, jnp.zeros_like(weighted)], axis=1)
    terms = jnp.zeros((rows, steps, cells), jnp.float32)
    for block in range(own_count):
        window = lax.dynamic_slice_in_dim(later, lag_of[block], steps, 1)
        terms = terms + jnp.einsum(
            "rts,sc->rtc", window, green[block], preferred_element_type=jnp.float32
        )
    return lax.psum_scatter(terms, "lag", scatter_dimension=1, tiled=True)


def solution(mesh):
    in_specs = (P("lag", None, "cell"), P(None, None, "cell"), P(), P(), P())
    out_specs = P(None, "lag", "cell")
    return jax.shard_map(body, mesh=mesh, in_specs=in_specs, out_specs=out_specs, check_vma=False)
```

profile of v0, /device:TPU:2, one launch (start us, length us, event | category | flops | bytes accessed | tf_op | source)
XLA Modules:
  0.0 551.9 jit_solution(6812498945430603760)
XLA Ops:
  6.5 0.0 all-reduce.4.cloned.1.call-start
  6.5 0.9 copy.10
  7.4 0.1 reduce-window.9
  7.5 0.1 reduce
  7.6 0.1 pad_add_fusion
  7.7 0.1 dynamic_slice.51
  7.8 0.7 fusion.66
  18.6 1.4 fusion.16
  20.0 2.4 convolution_add_fusion.6
  22.5 0.0 copy-done.1
  22.5 0.0 copy-done
  22.5 2.5 convolution_add_fusion.5
  25.0 2.5 convolution_add_fusion.4
  27.6 2.5 convolution_add_fusion.3
  30.1 2.5 convolution_add_fusion.2
  32.6 2.6 convolution_add_fusion.1
  35.2 2.5 convolution_add_fusion
  37.8 0.0 all-reduce.4.cloned.1.call-update
  37.8 0.0 reduce-scatter.2.cloned.1.call-start
  53.0 459.9 %all-reduce.4.cloned.1.call-done = f32[8,48,640]{2,1,0:T(8,128)} async-done(((f32[8,48,640]{2,1,0:T(8,128)}), f32[8,48,640]{2,1,0:T(8,128)}) %all-reduce.4.cloned.1.call-update) | async-done | bytes 983056 | tf_op jit(solution)/shard_map/psum | solution.py:22
  512.9 1.7 divide_convert_fusion
  514.6 0.3 fusion
  515.0 0.3 convolution_add_fusion.13
  515.3 0.3 convolution_add_fusion.12
  515.7 0.3 convolution_add_fusion.11
  516.0 0.3 convolution_add_fusion.10
  516.4 0.3 convolution_add_fusion.9
  516.7 0.3 convolution_add_fusion.8
  517.1 0.3 convolution_add_fusion.7
  517.4 1.0 copy.11
  518.4 0.0 reduce-scatter.2.cloned.1.call-update
  518.4 26.7 %reduce-scatter.2.cloned.1.call-done = f32[8,12,256]{2,0,1:T(8,128)} async-done(((f32[8,48,256]{2,0,1:T(8,128)}), f32[8,12,256]{2,0,1:T(8,128)}) %reduce-scatter.2.cloned.1.call-update) | async-done | bytes 98320 | tf_op jit(solution)/shard_map/reduce_scatter | solution.py:32
  (5 shorter events, 0.0 us)
Async XLA Ops:
  6.5 15.9 %copy-start.1 = (bf16[8,640,256]{2,1,0:T(8,128)(2,1)S(1)}, bf16[8,640,256]{2,1,0:T(8,128)(2,1)}, u32[]{:S(2)}) copy-start(bf16[8,640,256]{2,1,0:T(8,128)(2,1)} %param.5) | copy-start | bytes 7864324
  6.5 15.9 %copy-start = (bf16[8,48,256]{2,1,0:T(8,128)(2,1)S(1)}, bf16[8,48,256]{2,1,0:T(8,128)(2,1)}, u32[]{:S(2)}) copy-start(bf16[8,48,256]{2,1,0:T(8,128)(2,1)} %param.6) | copy-start | bytes 589828
  6.5 506.4 %all-reduce.4.cloned.1.call-start = ((), (), s32[]{:S(2)}) async-start(), calls=%async_computation.1 | async-start | bytes 1966080 | tf_op jit(solution)/shard_map/psum | solution.py:22
  32.6 20.3 %copy-start.2 = (s32[640]{0:T(1024)S(1)}, s32[640]{0:T(1024)}, u32[]{:S(2)}) copy-start(s32[640]{0:T(1024)} %param.9) | copy-start | bytes 7684
  37.8 507.3 %reduce-scatter.2.cloned.1.call-start = ((), (), s32[]{:S(2)}) async-start(), calls=%async_computation.2 | async-start | bytes 491520 | tf_op jit(solution)/shard_map/reduce_scatter | solution.py:32
Sparse Core Ops, SparseCore 0:
  37.9 474.9 all-reduce.3
  518.5 26.5 reduce-scatter.1
where the time goes:
time: 553 us; the launch traced here: 552 us
  waiting for transfers between devices  487 us (88%)
  between operations  38.8 us (7%)
  matrix products  21.9 us (4%)
    psum x1, waiting for transfers between devices, body(): summed = lax.psum(predicted, ('cell', 'lag'))  460 us
    reduce_scatter x1, waiting for transfers between devices, body(): return lax.psum_scatter(terms, 'lag', scatter_dimension=1, tiled=True)  26.7 us
    dot_general x8, matrix products, body(): jnp.einsum('rtc,sc->rts', shifted, green[block], preferred_element_type=j...  19.1 us
  transfers between devices with their start and end apart: 2, of which 2 were waited for; matrix products, arithmetic and copies ran while one was open for 0% of the time, Pallas kernels for 0%

commit v1 on v0

--- a/solution.py
+++ b/solution.py
@@ -19,7 +19,9 @@
             "rtc,sc->rts", shifted, green[block], preferred_element_type=jnp.float32
         )
     threshold = 0.3 * (huber_level.astype(jnp.float32) + 1.0)
-    summed = lax.psum(predicted, ("cell", "lag"))
+    summed = predicted
+    for axis in ("cell", "lag"):
+        summed = lax.psum(summed, axis)
     misfit = summed - observed
     weighted = (misfit * threshold / jnp.maximum(jnp.abs(misfit), threshold)).astype(jnp.bfloat16)
     later = jnp.concatenate([weighted, jnp.zeros_like(weighted)], axis=1)

time: 553 us -> 491 us (0.89)
  the two profiles are of different devices: /device:TPU:2 before, /device:TPU:4 now
where the time goes in v1:
time: 491 us; the launch traced here: 490 us
  waiting for transfers between devices  425 us (87%)
  between operations  38.5 us (8%)
  matrix products  21.9 us (4%)
    psum x2, waiting for transfers between devices, body(): summed = lax.psum(summed, axis)  395 us
    reduce_scatter x1, waiting for transfers between devices, body(): return lax.psum_scatter(terms, 'lag', scatter_dimension=1, tiled=True)  30.1 us
    dot_general x8, matrix products, body(): jnp.einsum('rtc,sc->rts', shifted, green[block], preferred_element_type=j...  19.2 us
  transfers between devices with their start and end apart: 3, of which 3 were waited for; matrix products, arithmetic and copies ran while one was open for 0% of the time, Pallas kernels for 0%

profile of v1, /device:TPU:4, one launch (start us, length us, event | category | flops | bytes accessed | tf_op | source)
XLA Modules:
  0.0 490.0 jit_solution(1034769991848796646)
XLA Ops:
  6.5 0.9 copy.10
  7.4 0.1 reduce-window.9
  7.5 0.1 reduce
  7.6 0.1 pad_add_fusion
  7.7 0.1 dynamic_slice.51
  7.8 0.7 fusion.66
  18.6 1.4 fusion.16
  20.0 2.4 convolution_add_fusion.6
  22.5 2.5 convolution_add_fusion.5
  25.0 2.5 convolution_add_fusion.4
  27.6 2.5 convolution_add_fusion.3
  30.1 2.5 convolution_add_fusion.2
  32.6 2.5 convolution_add_fusion.1
  35.2 2.6 convolution_add_fusion
  37.8 0.0 all-reduce.5.cloned.1.call-update
  37.8 0.0 all-reduce.7.cloned.1.call-start
  37.8 347.8 %all-reduce.5.cloned.1.call-done = f32[8,48,640]{2,1,0:T(8,128)} async-done(((f32[8,48,640]{2,1,0:T(8,128)}), f32[8,48,640]{2,1,0:T(8,128)}) %all-reduce.5.cloned.1.call-update) | async-done | bytes 983056 | tf_op jit(solution)/shard_map/psum | solution.py:24
  385.7 0.0 all-reduce.7.cloned.1.call-update
  385.7 0.0 reduce-scatter.2.cloned.1.call-start
  400.9 47.0 %all-reduce.7.cloned.1.call-done = f32[8,48,640]{2,1,0:T(8,128)} async-done(((f32[8,48,640]{2,1,0:T(8,128)}), f32[8,48,640]{2,1,0:T(8,128)}) %all-reduce.7.cloned.1.call-update) | async-done | bytes 983056 | tf_op jit(solution)/shard_map/psum | solution.py:24
  447.9 1.7 divide_convert_fusion
  449.6 0.3 fusion
  450.0 0.3 convolution_add_fusion.13
  450.4 0.3 convolution_add_fusion.12
  450.7 0.3 convolution_add_fusion.11
  451.1 0.3 convolution_add_fusion.10
  451.4 0.3 convolution_add_fusion.9
  451.8 0.3 convolution_add_fusion.8
  452.1 0.3 convolution_add_fusion.7
  452.4 1.0 copy.11
  453.4 0.0 reduce-scatter.2.cloned.1.call-update
  453.4 30.1 %reduce-scatter.2.cloned.1.call-done = f32[8,12,256]{2,0,1:T(8,128)} async-done(((f32[8,48,256]{2,0,1:T(8,128)}), f32[8,12,256]{2,0,1:T(8,128)}) %reduce-scatter.2.cloned.1.call-update) | async-done | bytes 98320 | tf_op jit(solution)/shard_map/reduce_scatter | solution.py:34
  (8 shorter events, 0.0 us)
Async XLA Ops:
  6.5 15.9 %copy-start.1 = (bf16[8,640,256]{2,1,0:T(8,128)(2,1)S(1)}, bf16[8,640,256]{2,1,0:T(8,128)(2,1)}, u32[]{:S(2)}) copy-start(bf16[8,640,256]{2,1,0:T(8,128)(2,1)} %param.5) | copy-start | bytes 7864324
  6.5 15.9 %copy-start = (bf16[8,48,256]{2,1,0:T(8,128)(2,1)S(1)}, bf16[8,48,256]{2,1,0:T(8,128)(2,1)}, u32[]{:S(2)}) copy-start(bf16[8,48,256]{2,1,0:T(8,128)(2,1)} %param.6) | copy-start | bytes 589828
  6.5 379.1 %all-reduce.5.cloned.1.call-start = ((), (), s32[]{:S(2)}) async-start(), calls=%async_computation.1 | async-start | bytes 1966080 | tf_op jit(solution)/shard_map/psum | solution.py:24
  35.2 365.7 %copy-start.2 = (s32[640]{0:T(1024)S(1)}, s32[640]{0:T(1024)}, u32[]{:S(2)}) copy-start(s32[640]{0:T(1024)} %param.9) | copy-start | bytes 7684
  37.8 410.2 %all-reduce.7.cloned.1.call-start = ((), (), s32[]{:S(2)}) async-start(), calls=%async_computation.2 | async-start | bytes 1966080 | tf_op jit(solution)/shard_map/psum | solution.py:24
  385.7 97.8 %reduce-scatter.2.cloned.1.call-start = ((), (), s32[]{:S(2)}) async-start(), calls=%async_computation.3 | async-start | bytes 491520 | tf_op jit(solution)/shard_map/reduce_scatter | solution.py:34
Sparse Core Ops, SparseCore 0:
  37.9 347.7 all-reduce.4
  388.1 59.8 all-reduce.6
  453.6 29.9 reduce-scatter.1
